TPU v7x, 512 devices: a whole 4x8x8 slice. The times are simulated.
512 devices in a mesh: row: 32 (over x, y), col: 16 (over z, core).
Axes of the slice: x: 4, y: 8, z: 8, core: 2. Of those that a mesh axis runs over, the one named last changes fastest.
Arguments:
- window: float32 [32, 2048, 16, 256], P('row', None, 'col'), may hold values from -7 to 8, as said below
Outputs:
- factored: float32 [32, 2048, 16, 256], P('row', None, 'col')
Inputs may be any that keep to these rules, and one draw needn't show every extreme that they name: `window`: entries above the diagonal are never read. The leading 2 * 128 by 256 block (lower triangle mirrored) is positive definite, with smallest eigenvalue 1 or more.
All inputs are finite; a program needn't handle non-finite values.
Results may differ from a plain program's by a relative error of at most 0.00028.
Values sent between devices are 32-bit elements; how exact they have to be, the bound alone decides.
A program may use at most 64 MiB of HBM per device.

v0:
```python
import jax
import jax.numpy as jnp
from jax import lax
from jax.sharding import PartitionSpec as P

NB = 128


def unmix_cols(gathered, col_count):
    height = gathered.shape[0]
    width = gathered.shape[1]
    return (
        gathered.reshape(height, col_count, width // col_count)
        .transpose(0, 2, 1)
        .reshape(height, width)
    )


def solve_rows(factor, rows_in):
    return jax.scipy.linalg.solve_triangular(factor, rows_in.T, lower=True).T


def body(window):
    blocks = window[0, :, 0, :]
    local_rows = blocks.shape[0]
    local_cols = blocks.shape[1]
    row_count = lax.axis_size("row")
    col_count = lax.axis_size("col")
    row_index = lax.axis_index("row")
    col_index = lax.axis_index("col")
    tile_height = NB // row_count
    tile_width = NB // col_count
    head_rows = local_cols * col_count // row_count
    groups = row_count // col_count
    for panel_step in range(2):
        first_col = panel_step * tile_width
        after_col = first_col + tile_width
        first_row = panel_step * tile_height
        tile_piece = blocks[first_row : first_row + tile_height, first_col:after_col]
        tile_wide = lax.all_gather(tile_piece, "col", axis=1, tiled=True)
        tile_full = lax.all_gather(tile_wide, "row", axis=0, tiled=True)
        tile_full = tile_full.reshape(row_count, tile_height, NB).transpose(1, 0, 2).reshape(NB, NB)
        diag_tile = unmix_cols(tile_full, col_count)
        symmetric = jnp.tril(diag_tile) + jnp.tril(diag_tile, -1).T
        factor = jnp.tril(jnp.linalg.cholesky(symmetric))
        panel_mine = blocks[:, first_col:after_col]
        gathered = lax.all_gather(panel_mine, "col", axis=1, tiled=True)
        solved = solve_rows(factor, unmix_cols(gathered, col_count))
        diag_rows = lax.dynamic_index_in_dim(
            factor.reshape(tile_height, row_count, NB), row_index, 1, False
        )
        panel_rows = jnp.concatenate(
            [jnp.zeros((first_row, NB), jnp.float32), diag_rows, solved[first_row + tile_height :]],
            0,
        )
        own_cols = lax.dynamic_index_in_dim(
            panel_rows.reshape(local_rows, tile_width, col_count), col_index, 2, False
        )
        sending = panel_rows[:head_rows]
        all_rows = lax.all_gather(sending, "row", axis=0, tiled=True)
        picked = lax.dynamic_index_in_dim(
            all_rows.reshape(groups, col_count, head_rows, NB), col_index, 1, False
        )
        col_rows = picked.transpose(1, 0, 2).reshape(local_cols, NB)
        update = jnp.dot(panel_rows, col_rows[after_col:].T, precision=lax.Precision.HIGHEST)
        trailing = blocks[:, after_col:] - update
        blocks = jnp.concatenate([blocks[:, :first_col], own_cols, trailing], 1)
    global_rows = jnp.arange(local_rows)[:, None] * row_count + row_index
    global_cols = jnp.arange(local_cols)[None, :] * col_count + col_index
    lower_mask = global_rows >= global_cols
    result = jnp.where(lower_mask, blocks, 0.0)
    return result[None, :, None, :]


def solution(mesh):
    in_specs = (P("row", None, "col", None),)
    out_specs = P("row", None, "col", None)
    return jax.shard_map(body, mesh=mesh, in_specs=in_specs, out_specs=out_specs, check_vma=False)
```

profile of v0, /device:TPU:14, one launch (start us, length us, event | category | flops | bytes accessed | tf_op | source)
XLA Modules:
  0.0 380.1 jit_solution(15478815313496594066)
XLA Ops:
  6.5 4.6 %copy.51 = f32[1,2048,1,256]{1,3,2,0:T(8,128)S(1)} copy(f32[1,2048,1,256]{3,2,1,0:T(1,128)} %param.4) | data formatting | bytes 4194304 | tf_op args[0]
  11.1 0.6 slice.65
  11.9 23.2 %all-gather = f32[16,8,4]{1,2,0:T(4,128)S(1)} all-gather(f32[1,8,4]{1,2,0:T(4,128)S(1)} %bitcast.136), channel_id=1, replica_groups=mesh['row'=32,'col'=16] {'col'}, dimensions={0}, use_global_device_ids=true | all-gather | bytes 2176 | tf_op jit(solution)/shard_map/all_gather | solution.py:40
  35.1 0.1 reshape.171
  35.2 48.2 %all-gather.1 = f32[32,4,128]{2,1,0:T(4,128)S(1)} all-gather(f32[1,4,128]{2,1,0:T(4,128)S(1)} %bitcast.137), channel_id=1, replica_groups=mesh['row'=32,'col'=16] {'row'}, dimensions={0}, use_global_device_ids=true | all-gather | bytes 67584 | tf_op jit(solution)/shard_map/all_gather | solution.py:41
  83.4 0.2 copy.54
  83.6 0.2 reshape_reshape.6
  83.7 0.1 copy.57
  83.9 0.1 bitcast_add_fusion.3
  83.9 0.1 copy.58
  84.1 11.7 %cholesky.44 = f32[128,128]{1,0:T(8,128)S(1)} custom-call(f32[128,128]{1,0:T(8,128)S(1)} %fusion.8), custom_call_target="Cholesky" | custom-call | tf_op jit(solution)/shard_map/jit(cholesky)/cholesky | solution.py:45
  95.8 0.1 copy.59
  95.9 0.1 select_reduce_fusion.1
  96.0 0.7 compare_reduce_fusion.1
  96.7 0.6 select_bitcast_fusion.1
  97.3 0.1 copy.62
  97.5 0.1 copy.66
  97.6 0.1 copy.63
  97.7 9.8 %custom-call.6 = f32[1,128,128]{1,2,0:T(8,128)S(1)} custom-call(f32[1,128,128]{2,1,0:T(8,128)S(1)} %copy.63), custom_call_target="InvertDiagBlocksLowerTriangular" | custom-call | tf_op jit(solution)/shard_map/jit(_solve_triangular)/triangular_solve | solution.py:20
  107.5 1.8 copy.64
  109.4 1.1 convolution_bitcast_fusion.1
  110.4 0.3 slice.66
  110.7 0.7 pad_maximum_fusion
  111.5 76.0 %all-gather.11.cloned.1.call-done = f32[4096,128]{0,1:T(8,128)} async-done(((f32[128,128]{0,1:T(8,128)}), f32[4096,128]{0,1:T(8,128)}) %all-gather.11.cloned.1.call-update) | async-done | bytes 2097168 | tf_op jit(solution)/shard_map/all_gather | solution.py:60
  187.6 2.0 copy.88
  189.5 0.1 constant_dynamic-slice_fusion.2
  189.7 0.1 copy.67
  189.8 1.9 convolution_subtract_fusion
  191.7 1.3 copy-done
  193.0 0.6 slice.70
  193.7 0.2 all-gather.15.cloned.1.call-start
  193.9 0.1 copy.75
  194.0 0.8 slice_bitcast_fusion
  194.8 0.1 copy.68
  194.9 18.1 %all-gather.2 = f32[16,8,4]{1,2,0:T(4,128)S(1)} all-gather(f32[1,8,4]{1,2,0:T(4,128)S(1)} %bitcast.138), channel_id=1, replica_groups=mesh['row'=32,'col'=16] {'col'}, dimensions={0}, use_global_device_ids=true | all-gather | bytes 2176 | tf_op jit(solution)/shard_map/all_gather | solution.py:40
  213.0 0.1 reshape.175
  213.1 46.1 %all-gather.3 = f32[32,4,128]{2,1,0:T(4,128)S(1)} all-gather(f32[1,4,128]{2,1,0:T(4,128)S(1)} %bitcast.139), channel_id=1, replica_groups=mesh['row'=32,'col'=16] {'row'}, dimensions={0}, use_global_device_ids=true | all-gather | bytes 67584 | tf_op jit(solution)/shard_map/all_gather | solution.py:41
  259.2 0.2 copy.70
  259.4 0.2 reshape_reshape.7
  259.6 0.1 copy.73
  259.7 0.1 bitcast_add_fusion.1
  259.8 0.1 copy.74
  259.9 11.7 %cholesky.55 = f32[128,128]{1,0:T(8,128)S(1)} custom-call(f32[128,128]{1,0:T(8,128)S(1)} %fusion.6), custom_call_target="Cholesky" | custom-call | tf_op jit(solution)/shard_map/jit(cholesky)/cholesky | solution.py:45
  271.6 0.6 compare_reduce_fusion
  272.3 0.6 select_bitcast_fusion
  272.8 9.8 %custom-call.7 = f32[1,128,128]{1,2,0:T(8,128)S(1)} custom-call(f32[1,128,128]{2,1,0:T(8,128)S(1)} %get-tuple-element.6), custom_call_target="InvertDiagBlocksLowerTriangular" | custom-call | tf_op jit(solution)/shard_map/jit(_solve_triangular)/triangular_solve | solution.py:20
  282.7 0.1 copy.80
  282.8 1.8 copy.77
  284.7 1.1 convolution_bitcast_fusion
  285.7 0.3 slice.71
  286.1 1.0 concatenate.45
  287.0 0.7 slice.73
  287.7 0.1 copy.83
  287.9 0.2 fusion.4
  288.2 0.1 copy.78
  288.3 0.6 copy.79
  288.9 0.7 concatenate.43
  289.7 75.8 %all-gather.15.cloned.1.call-done = f32[4096,128]{0,1:T(8,128)} async-done(((f32[128,128]{0,1:T(8,128)}), f32[4096,128]{0,1:T(8,128)}) %all-gather.15.cloned.1.call-update) | async-done | bytes 2097168 | tf_op jit(solution)/shard_map/all_gather | solution.py:60
  365.5 2.1 copy.89
  367.6 0.1 constant_dynamic-slice_fusion
  367.8 0.1 copy.81
  368.0 1.8 fusion
  369.8 0.2 maximum_select_fusion
  370.0 3.6 copy.82
  (37 shorter events, 0.6 us)
Async XLA Ops:
  6.5 101.0 %all-gather.9.cloned.1.call-start = ((), (), s32[]{:S(2)}) async-start(), calls=%async_computation | async-start | bytes 1114112 | tf_op jit(solution)/shard_map/all_gather | solution.py:47
  11.8 175.8 %all-gather.11.cloned.1.call-start = ((), (), s32[]{:S(2)}) async-start(), calls=%async_computation.1 | async-start | bytes 2162688 | tf_op jit(solution)/shard_map/all_gather | solution.py:60
  111.5 171.3 %all-gather.13.cloned.1.call-start = ((), (), s32[]{:S(2)}) async-start(), calls=%async_computation.2 | async-start | bytes 1114112 | tf_op jit(solution)/shard_map/all_gather | solution.py:47
  191.7 1.3 copy-start
  193.7 171.9 %all-gather.15.cloned.1.call-start = ((), (), s32[]{:S(2)}) async-start(), calls=%async_computation.3 | async-start | bytes 2162688 | tf_op jit(solution)/shard_map/all_gather | solution.py:60
  287.0 2.6 copy-start.2
  365.5 2.4 copy-start.1
  365.5 2.5 copy-start.3
Sparse Core Ops, SparseCore 0:
  11.9 46.4 all-gather.8
  111.6 75.8 all-gather.10
  193.8 41.1 all-gather.12
  287.9 77.6 all-gather.14
where the time goes:
time: 380 us
  waiting for transfers between devices  152 us (40%)
  blocking collectives  136 us (36%)
  other arithmetic  47.1 us (12%)
  local copies, waits for them, and re-layouts  25.8 us (7%)
  between operations  13.6 us (4%)
  matrix products  5.78 us (2%)
    all_gather x2, waiting for transfers between devices, body(): all_rows = lax.all_gather(sending, 'row', axis=0, tiled=True)  152 us
    all_gather x2, blocking collectives, body(): tile_full = lax.all_gather(tile_wide, 'row', axis=0, tiled=True)  94.3 us
    all_gather x2, blocking collectives, body(): tile_wide = lax.all_gather(tile_piece, 'col', axis=1, tiled=True)  41.3 us
    another operation x6, other arithmetic, body(): factor = jnp.tril(jnp.linalg.cholesky(symmetric))  24.9 us
    another operation x4, other arithmetic, solve_rows(): return jax.scipy.linalg.solve_triangular(factor, rows_in.T, lower=True).T  20.8 us
    unnamed x18, local copies, waits for them, and re-layouts  11.1 us
  transfers between devices with their start and end apart: 4, of which 2 were waited for; matrix products, arithmetic and copies ran while one was open for 13% of the time, Pallas kernels for 0%

commit v1 on v0

--- a/solution.py
+++ b/solution.py
@@ -38,7 +38,9 @@
         first_row = panel_step * tile_height
         tile_piece = blocks[first_row : first_row + tile_height, first_col:after_col]
         tile_wide = lax.all_gather(tile_piece, "col", axis=1, tiled=True)
-        tile_full = lax.all_gather(tile_wide, "row", axis=0, tiled=True)
+        s_next = jnp.stack([tile_wide for _ in range(lax.axis_size("row"))])
+        q_next = lax.all_to_all(s_next, "row", 0, 0)
+        tile_full = jnp.concatenate(q_next, axis=0)
         tile_full = tile_full.reshape(row_count, tile_height, NB).transpose(1, 0, 2).reshape(NB, NB)
         diag_tile = unmix_cols(tile_full, col_count)
         symmetric = jnp.tril(diag_tile) + jnp.tril(diag_tile, -1).T

time: 380 us -> 314 us (0.83)
  blocking collectives: 136 us -> 41.3 us
  starting transfers between devices: 0.31 us -> 18.2 us
  waiting for transfers between devices: 152 us -> 161 us
    all_gather x2 -> x0, blocking collectives: 94.3 us -> none  [body(): tile_full = lax.all_gather(tile_wide, 'row', axis=0, tiled=True)]
    all_to_all x0 -> x2, starting transfers between devices: none -> 17.9 us  [body(): q_next = lax.all_to_all(s_next, 'row', 0, 0)]
    all_to_all x0 -> x2, waiting for transfers between devices: none -> 15 us  [body(): q_next = lax.all_to_all(s_next, 'row', 0, 0)]
    all_gather x2, waiting for transfers between devices: 152 us -> 146 us  [body(): all_rows = lax.all_gather(sending, 'row', axis=0, tiled=True)]
  transfers between devices with their start and end apart: 4 -> 6, of which waited for: 2 -> 4; matrix products, arithmetic and copies ran while one was open for 13% -> 17% of each run, Pallas kernels for 0% -> 0%
where the time goes in v1:
time: 314 us
  waiting for transfers between devices  161 us (51%)
  other arithmetic  47.1 us (15%)
  blocking collectives  41.3 us (13%)
  local copies, waits for them, and re-layouts  27.1 us (9%)
  starting transfers between devices  18.2 us (6%)
  between operations  13.6 us (4%)
  matrix products  5.77 us (2%)
    all_gather x2, waiting for transfers between devices, body(): all_rows = lax.all_gather(sending, 'row', axis=0, tiled=True)  146 us
    all_gather x2, blocking collectives, body(): tile_wide = lax.all_gather(tile_piece, 'col', axis=1, tiled=True)  41.3 us
    another operation x6, other arithmetic, body(): factor = jnp.tril(jnp.linalg.cholesky(symmetric))  24.9 us
    another operation x4, other arithmetic, solve_rows(): return jax.scipy.linalg.solve_triangular(factor, rows_in.T, lower=True).T  20.8 us
    all_to_all x2, starting transfers between devices, body(): q_next = lax.all_to_all(s_next, 'row', 0, 0)  17.9 us
    all_to_all x2, waiting for transfers between devices, body(): q_next = lax.all_to_all(s_next, 'row', 0, 0)  15 us
    unnamed x18, local copies, waits for them, and re-layouts  11.1 us
  transfers between devices with their start and end apart: 6, of which 4 were waited for; matrix products, arithmetic and copies ran while one was open for 17% of the time, Pallas kernels for 0%

profile of v1, /device:TPU:14, one launch (start us, length us, event | category | flops | bytes accessed | tf_op | source)
XLA Modules:
  0.0 313.7 jit_solution(1317068976124358734)
XLA Ops:
  6.5 4.6 %copy.53 = f32[1,2048,1,256]{1,3,2,0:T(8,128)S(1)} copy(f32[1,2048,1,256]{3,2,1,0:T(1,128)} %param.4) | data formatting | bytes 4194304 | tf_op args[0]
  11.1 0.6 slice.65
  11.9 23.2 %all-gather = f32[16,8,4]{1,2,0:T(4,128)S(1)} all-gather(f32[1,8,4]{1,2,0:T(4,128)S(1)} %bitcast.132), channel_id=1, replica_groups=mesh['row'=32,'col'=16] {'col'}, dimensions={0}, use_global_device_ids=true | all-gather | bytes 2176 | tf_op jit(solution)/shard_map/all_gather | solution.py:40
  35.1 0.1 reshape.167
  35.2 0.6 stack.4
  35.8 10.1 %all-to-all-start = ((f32[32,4,128]{2,1,0:T(4,128)}), f32[32,4,128]{2,1,0:T(4,128)S(1)}, u32[]{:S(2)}, u32[]{:S(2)}) async-start(f32[32,4,128]{2,1,0:T(4,128)} %stack.4), calls=%async_computation | async-start | bytes 131072 | tf_op jit(solution)/shard_map/all_to_all | solution.py:42
  46.0 7.6 %all-to-all-done = f32[32,4,128]{2,1,0:T(4,128)S(1)} async-done(((f32[32,4,128]{2,1,0:T(4,128)}), f32[32,4,128]{2,1,0:T(4,128)S(1)}, u32[]{:S(2)}, u32[]{:S(2)}) %all-to-all-start) | async-done | bytes 65568 | tf_op jit(solution)/shard_map/all_to_all | solution.py:42
  53.6 0.1 copy.56
  53.7 0.2 reshape_reshape.6
  54.0 0.1 bitcast_add_fusion.3
  54.2 11.7 %cholesky.44 = f32[128,128]{1,0:T(8,128)S(1)} custom-call(f32[128,128]{1,0:T(8,128)S(1)} %fusion.8), custom_call_target="Cholesky" | custom-call | tf_op jit(solution)/shard_map/jit(cholesky)/cholesky | solution.py:47
  65.9 0.1 copy.61
  66.0 0.1 select_reduce_fusion.1
  66.1 0.6 compare_reduce_fusion.1
  66.8 0.6 select_bitcast_fusion.1
  67.4 0.1 copy.64
  67.5 0.1 copy.68
  67.7 9.8 %custom-call.6 = f32[1,128,128]{1,2,0:T(8,128)S(1)} custom-call(f32[1,128,128]{2,1,0:T(8,128)S(1)} %copy.65), custom_call_target="InvertDiagBlocksLowerTriangular" | custom-call | tf_op jit(solution)/shard_map/jit(_solve_triangular)/triangular_solve | solution.py:20
  77.5 1.8 copy.66
  79.4 1.1 convolution_bitcast_fusion.1
  80.4 0.3 slice.66
  80.8 0.7 pad_maximum_fusion
  81.5 0.2 all-gather.11.cloned.1.call-start
  81.7 72.9 %all-gather.9.cloned.1.call-done = f32[4096,128]{0,1:T(8,128)} async-done(((f32[128,128]{0,1:T(8,128)}), f32[4096,128]{0,1:T(8,128)}) %all-gather.9.cloned.1.call-update) | async-done | bytes 2097168 | tf_op jit(solution)/shard_map/all_gather | solution.py:62
  154.7 2.0 copy.90
  156.6 0.1 constant_dynamic-slice_fusion.2
  156.8 0.1 copy.69
  156.9 1.9 convolution_subtract_fusion
  158.9 1.3 copy-done
  160.1 0.6 slice.70
  160.8 0.8 slice_bitcast_fusion
  161.6 18.1 %all-gather.1 = f32[16,8,4]{1,2,0:T(4,128)S(1)} all-gather(f32[1,8,4]{1,2,0:T(4,128)S(1)} %bitcast.134), channel_id=1, replica_groups=mesh['row'=32,'col'=16] {'col'}, dimensions={0}, use_global_device_ids=true | all-gather | bytes 2176 | tf_op jit(solution)/shard_map/all_gather | solution.py:40
  179.8 0.1 reshape.169
  179.9 0.6 stack.5
  180.5 7.7 %all-to-all-start.1 = ((f32[32,4,128]{2,1,0:T(4,128)}), f32[32,4,128]{2,1,0:T(4,128)S(1)}, u32[]{:S(2)}, u32[]{:S(2)}) async-start(f32[32,4,128]{2,1,0:T(4,128)} %stack.5), calls=%async_computation.1 | async-start | bytes 131072 | tf_op jit(solution)/shard_map/all_to_all | solution.py:42
  188.3 0.1 copy.77
  188.4 7.4 %all-to-all-done.1 = f32[32,4,128]{2,1,0:T(4,128)S(1)} async-done(((f32[32,4,128]{2,1,0:T(4,128)}), f32[32,4,128]{2,1,0:T(4,128)S(1)}, u32[]{:S(2)}, u32[]{:S(2)}) %all-to-all-start.1) | async-done | bytes 65568 | tf_op jit(solution)/shard_map/all_to_all | solution.py:42
  195.9 0.2 copy.72
  196.0 0.2 reshape_reshape.7
  196.2 0.1 copy.75
  196.3 0.1 bitcast_add_fusion.1
  196.4 0.1 copy.76
  196.5 11.7 %cholesky.55 = f32[128,128]{1,0:T(8,128)S(1)} custom-call(f32[128,128]{1,0:T(8,128)S(1)} %fusion.6), custom_call_target="Cholesky" | custom-call | tf_op jit(solution)/shard_map/jit(cholesky)/cholesky | solution.py:47
  208.2 0.7 compare_reduce_fusion
  208.9 0.6 select_bitcast_fusion
  209.6 9.8 %custom-call.7 = f32[1,128,128]{1,2,0:T(8,128)S(1)} custom-call(f32[1,128,128]{2,1,0:T(8,128)S(1)} %get-tuple-element.6), custom_call_target="InvertDiagBlocksLowerTriangular" | custom-call | tf_op jit(solution)/shard_map/jit(_solve_triangular)/triangular_solve | solution.py:20
  219.4 0.1 copy.82
  219.6 1.8 copy.79
  221.4 1.1 convolution_bitcast_fusion
  222.4 0.3 slice.71
  222.8 1.0 concatenate.45
  223.8 0.7 slice.73
  224.5 0.1 copy.85
  224.6 0.2 fusion.4
  224.9 0.1 copy.80
  225.0 0.6 copy.81
  225.7 0.7 concatenate.43
  226.4 72.6 %all-gather.13.cloned.1.call-done = f32[4096,128]{0,1:T(8,128)} async-done(((f32[128,128]{0,1:T(8,128)}), f32[4096,128]{0,1:T(8,128)}) %all-gather.13.cloned.1.call-update) | async-done | bytes 2097168 | tf_op jit(solution)/shard_map/all_gather | solution.py:62
  299.1 2.1 copy.91
  301.2 0.1 constant_dynamic-slice_fusion
  301.3 0.1 copy.83
  301.6 1.8 fusion
  303.3 0.2 maximum_select_fusion
  303.5 3.6 %copy.84 = f32[1,2048,1,256]{3,2,1,0:T(1,128)} copy(f32[1,2048,1,256]{1,3,2,0:T(8,128)S(1)} %maximum_select_fusion) | data formatting | bytes 4194304 | tf_op jit(solution)/shard_map/jit(_where)/select_n | solution.py:73
  (41 shorter events, 1.0 us)
Async XLA Ops:
  6.5 71.0 %all-gather.7.cloned.1.call-start = ((), (), s32[]{:S(2)}) async-start(), calls=%async_computation.2 | async-start | bytes 1114112 | tf_op jit(solution)/shard_map/all_gather | solution.py:49
  35.8 17.8 %all-to-all-start = ((f32[32,4,128]{2,1,0:T(4,128)}), f32[32,4,128]{2,1,0:T(4,128)S(1)}, u32[]{:S(2)}, u32[]{:S(2)}) async-start(f32[32,4,128]{2,1,0:T(4,128)} %stack.4), calls=%async_computation | async-start | bytes 131072 | tf_op jit(solution)/shard_map/all_to_all | solution.py:42
  45.9 108.7 %all-gather.9.cloned.1.call-start = ((), (), s32[]{:S(2)}) async-start(), calls=%async_computation.3 | async-start | bytes 2162688 | tf_op jit(solution)/shard_map/all_gather | solution.py:62
  81.5 138.0 %all-gather.11.cloned.1.call-start = ((), (), s32[]{:S(2)}) async-start(), calls=%async_computation.4 | async-start | bytes 1114112 | tf_op jit(solution)/shard_map/all_gather | solution.py:49
  158.8 1.3 copy-start
  180.5 15.4 %all-to-all-start.1 = ((f32[32,4,128]{2,1,0:T(4,128)}), f32[32,4,128]{2,1,0:T(4,128)S(1)}, u32[]{:S(2)}, u32[]{:S(2)}) async-start(f32[32,4,128]{2,1,0:T(4,128)} %stack.5), calls=%async_computation.1 | async-start | bytes 131072 | tf_op jit(solution)/shard_map/all_to_all | solution.py:42
  188.2 110.9 %all-gather.13.cloned.1.call-start = ((), (), s32[]{:S(2)}) async-start(), calls=%async_computation.5 | async-start | bytes 2162688 | tf_op jit(solution)/shard_map/all_gather | solution.py:62
  223.8 2.6 copy-start.2
  299.1 2.4 copy-start.1
  299.1 2.5 copy-start.3
Sparse Core Ops, SparseCore 0:
  11.9 46.4 all-gather.6
  81.6 73.0 all-gather.8
  160.9 41.1 all-gather.10
  224.6 74.4 all-gather.12
